TPU v7x, 32 devices: a whole 2x2x4 slice. The times are simulated.
32 devices in a mesh: dp: 16 (over z, y, core), mp: 2 (over x).
Axes of the slice: x: 2, y: 2, z: 4, core: 2. Of those that a mesh axis runs over, the one named last changes fastest.
Arguments:
- layer_input: bfloat16 [24576, 768], P(('dp', 'mp')), may hold values from -6 to 6
- gain_attn: bfloat16 [768], replicated, may hold values from 0.5 to 1.5
- w_query: bfloat16 [768, 768], P(None, 'mp'), may hold values from -0.3125 to 0.3125
- w_key: bfloat16 [768, 768], P(None, 'mp'), may hold values from -0.21875 to 0.21875
- w_value: bfloat16 [768, 768], P(None, 'mp'), may hold values from -0.21875 to 0.21875
- w_out: bfloat16 [768, 768], P('mp'), may hold values from -0.875 to 0.875
- gain_mlp: bfloat16 [768], replicated, may hold values from 0.5 to 1.5
- w_gate: bfloat16 [768, 2048], P(None, 'mp'), may hold values from -0.21875 to 0.21875
- w_up: bfloat16 [768, 2048], P(None, 'mp'), may hold values from -0.21875 to 0.21875
- w_down: bfloat16 [2048, 768], P('mp'), may hold values from -0.125 to 0.125
- segment_start: int32 [16, 7], P('dp'), may hold values from 0 to 1472, as said below
- segment_parent: int32 [16, 7], P('dp'), may hold values from 0 to 2, as said below
- out_grad: bfloat16 [24576, 768], P(('dp', 'mp')), may hold values from -6 to 6
Outputs:
- output: float32 [24576, 768], P(('dp', 'mp'))
- input_grad: float32 [24576, 768], P(('dp', 'mp'))
- gain_attn_grad: float32 [768], replicated
- w_query_grad: float32 [768, 768], P(None, 'mp')
- w_key_grad: float32 [768, 768], P(None, 'mp')
- w_value_grad: float32 [768, 768], P(None, 'mp')
- w_out_grad: float32 [768, 768], P('mp')
- gain_mlp_grad: float32 [768], replicated
- w_gate_grad: float32 [768, 2048], P(None, 'mp')
- w_up_grad: float32 [768, 2048], P(None, 'mp')
- w_down_grad: float32 [2048, 768], P('mp')
Inputs may be any that keep to these rules, and one draw needn't show every extreme that they name: `segment_start`: per tree the segments are stored in order trunk, two branches, four leaves; starts rise strictly from 0, every branch or leaf has 64 to 192 tokens, and the last leaf has exactly 64. `segment_parent`: segment 0 is the trunk (entry 0), segments 1 and 2 have parent 0, and each of them is the parent of exactly two of segments 3 to 6.
All inputs are finite; a program needn't handle non-finite values.
Results may differ from a plain program's by a relative error of at most 0.018.
Values may be sent and summed in bfloat16 or wider, within the bound.
A program may use at most 192 MiB of HBM per device.

v0:
```python
import jax
import jax.numpy as jnp
from jax import lax
from jax.sharding import PartitionSpec as P

HD = 64


EPSILON = 1e-05
ROPE_BASE = 10000.0


def tree_tables(starts, parents, length):
    seg_count = starts.shape[0]
    tok_index = jnp.arange(length, dtype=jnp.int32)
    labels = jnp.arange(seg_count, dtype=jnp.int32)
    segment = jnp.sum(
        (tok_index[:, None] >= starts[None, 1:]).astype(jnp.int32), axis=1, dtype=jnp.int32
    )
    seg_ends = jnp.concatenate([starts[1:], jnp.full((1,), length, dtype=jnp.int32)])
    seg_lengths = seg_ends - starts
    same_seg = (labels[:, None] == labels[None, :]).astype(jnp.int32)
    parent_hot = (parents[:, None] == labels[None, :]).astype(jnp.int32)
    reaches = same_seg + parent_hot + jnp.dot(parent_hot, parent_hot)
    ancestry = (reaches > 0).astype(jnp.int32)
    offset = jnp.dot(ancestry * (1 - same_seg), seg_lengths)
    onehot = (segment[:, None] == labels[None, :]).astype(jnp.int32)
    position = tok_index - jnp.dot(onehot, starts) + jnp.dot(onehot, offset)
    visible = jnp.dot(onehot, ancestry)
    return (position, visible, onehot)


def rotary_tables(position, head_size):
    half_size = head_size // 2
    inv_freq = ROPE_BASE ** (-2.0 * jnp.arange(half_size, dtype=jnp.float32) / head_size)
    angles = position.astype(jnp.float32)[:, None] * inv_freq[None, :]
    return (jnp.cos(angles), jnp.sin(angles))


def rotate(vectors, cosine, sine_tab):
    half_size = vectors.shape[-1] // 2
    first_half = vectors[..., :half_size]
    second = vectors[..., half_size:]
    cos_b = cosine[:, None, :]
    sin_b = sine_tab[:, None, :]
    return jnp.concatenate(
        [first_half * cos_b - second * sin_b, second * cos_b + first_half * sin_b], axis=-1
    )


def rotate_back(gradient, cosine, sine_tab):
    half_size = gradient.shape[-1] // 2
    first_half = gradient[..., :half_size]
    second = gradient[..., half_size:]
    cos_b = cosine[:, None, :]
    sin_b = sine_tab[:, None, :]
    return jnp.concatenate(
        [first_half * cos_b + second * sin_b, second * cos_b - first_half * sin_b], axis=-1
    )


def contract_last(left_mat, right_mat):
    return lax.dot_general(
        left_mat, right_mat, (((1,), (1,)), ((), ())), preferred_element_type=jnp.float32
    )


def inner_rows(left_mat, right_mat):
    return lax.dot_general(
        left_mat, right_mat, (((0,), (0,)), ((), ())), preferred_element_type=jnp.float32
    )


def rms_scale(vectors):
    return lax.rsqrt(jnp.mean(vectors * vectors, axis=-1, keepdims=True) + EPSILON)


def on_device(
    layer_input,
    gain_attn,
    w_query,
    w_key,
    w_value,
    w_out,
    gain_mlp,
    w_gate,
    w_up,
    w_down,
    segment_start,
    segment_parent,
    out_grad,
):
    tok_rows = layer_input.shape[0]
    tree_len = tok_rows * lax.axis_size("mp")
    local_heads = w_query.shape[1] // HD
    score_scale = HD ** (-0.5)
    position, visible, onehot = tree_tables(segment_start[0], segment_parent[0], tree_len)
    cosine, sine_tab = rotary_tables(position, HD)
    block_rows = min(512, tree_len)
    block_starts = jnp.arange(tree_len // block_rows, dtype=jnp.int32) * block_rows
    key_index = jnp.arange(tree_len, dtype=jnp.int32)

    def block_mask(first_row):
        vis_block = lax.dynamic_slice_in_dim(visible, first_row, block_rows, 0)
        q_index = first_row + jnp.arange(block_rows, dtype=jnp.int32)
        return (jnp.dot(vis_block, onehot.T) > 0) & (key_index[None, :] <= q_index[:, None])

    inputs_f32 = layer_input.astype(jnp.float32)
    inv_one = rms_scale(inputs_f32)
    normed = (inputs_f32 * inv_one * gain_attn).astype(jnp.bfloat16)
    normed_all = lax.all_gather(normed, "mp", axis=0, tiled=True)
    q_pre = jnp.dot(normed_all, w_query, preferred_element_type=jnp.float32)
    k_pre = jnp.dot(normed_all, w_key, preferred_element_type=jnp.float32)
    values = jnp.dot(normed_all, w_value, preferred_element_type=jnp.float32).astype(jnp.bfloat16)
    values = values.reshape(tree_len, local_heads, HD)
    query = rotate(q_pre.reshape(tree_len, local_heads, HD), cosine, sine_tab).astype(jnp.bfloat16)
    key_rot = rotate(k_pre.reshape(tree_len, local_heads, HD), cosine, sine_tab).astype(
        jnp.bfloat16
    )

    def attend(first_row):
        q_block = lax.dynamic_slice_in_dim(query, first_row, block_rows, 0)
        scores = (
            jnp.einsum("qhd,khd->hqk", q_block, key_rot, preferred_element_type=jnp.float32)
            * score_scale
        )
        masked = jnp.where(block_mask(first_row)[None], scores, -1e30)
        row_max = jnp.max(masked, axis=-1, keepdims=True)
        exp_terms = jnp.exp(masked - row_max)
        row_sum = jnp.sum(exp_terms, axis=-1, keepdims=True)
        prob_rows = (exp_terms / row_sum).astype(jnp.bfloat16)
        head_out = jnp.einsum("hqk,khd->qhd", prob_rows, values, preferred_element_type=jnp.float32)
        return (head_out.astype(jnp.bfloat16), row_max[..., 0] + jnp.log(row_sum[..., 0]))

    head_blocks, lse_blocks = lax.map(attend, block_starts)
    heads_out = head_blocks.reshape(tree_len, local_heads * HD)
    attn_out = lax.psum_scatter(
        jnp.dot(heads_out, w_out, preferred_element_type=jnp.float32).astype(jnp.bfloat16),
        "mp",
        scatter_dimension=0,
        tiled=True,
    ).astype(jnp.float32)
    residual = inputs_f32 + attn_out
    inv_two = rms_scale(residual)
    normed_two = (residual * inv_two * gain_mlp).astype(jnp.bfloat16)
    normed_two_all = lax.all_gather(normed_two, "mp", axis=0, tiled=True)
    gate_pre = jnp.dot(normed_two_all, w_gate, preferred_element_type=jnp.float32)
    up_pre = jnp.dot(normed_two_all, w_up, preferred_element_type=jnp.float32)
    sigmoid_gate = jax.nn.sigmoid(gate_pre)
    silu_gate = gate_pre * sigmoid_gate
    hidden = (silu_gate * up_pre).astype(jnp.bfloat16)
    output = residual + lax.psum_scatter(
        jnp.dot(hidden, w_down, preferred_element_type=jnp.float32).astype(jnp.bfloat16),
        "mp",
        scatter_dimension=0,
        tiled=True,
    ).astype(jnp.float32)
    grads_all = lax.all_gather(out_grad, "mp", axis=0, tiled=True)
    grad_down = inner_rows(hidden, grads_all)
    d_hidden = contract_last(grads_all, w_down)
    d_gate = (d_hidden * up_pre * sigmoid_gate * (1.0 + gate_pre * (1.0 - sigmoid_gate))).astype(
        jnp.bfloat16
    )
    d_up = (d_hidden * silu_gate).astype(jnp.bfloat16)
    grad_gate = inner_rows(normed_two_all, d_gate)
    grad_up = inner_rows(normed_two_all, d_up)
    d_norm_two = lax.psum_scatter(
        (contract_last(d_gate, w_gate) + contract_last(d_up, w_up)).astype(jnp.bfloat16),
        "mp",
        scatter_dimension=0,
        tiled=True,
    ).astype(jnp.float32)
    scaled_two = gain_mlp * d_norm_two
    gain_mlp_part = jnp.sum(d_norm_two * residual * inv_two, axis=0)
    d_resid = (
        out_grad.astype(jnp.float32)
        + inv_two * scaled_two
        - residual * inv_two**3 * jnp.mean(scaled_two * residual, axis=-1, keepdims=True)
    )
    d_attn_all = lax.all_gather(d_resid.astype(jnp.bfloat16), "mp", axis=0, tiled=True)
    grad_out = inner_rows(heads_out, d_attn_all)
    d_heads = (
        contract_last(d_attn_all, w_out).astype(jnp.bfloat16).reshape(tree_len, local_heads, HD)
    )

    def attend_back(sums_in, block_items):
        key_acc, value_acc = sums_in
        first_row, lse_block = block_items
        q_block = lax.dynamic_slice_in_dim(query, first_row, block_rows, 0)
        d_block = lax.dynamic_slice_in_dim(d_heads, first_row, block_rows, 0)
        scores = (
            jnp.einsum("qhd,khd->hqk", q_block, key_rot, preferred_element_type=jnp.float32)
            * score_scale
        )
        masked = jnp.where(block_mask(first_row)[None], scores, -1e30)
        prob_rows = jnp.exp(masked - lse_block[..., None])
        d_probs = jnp.einsum("qhd,khd->hqk", d_block, values, preferred_element_type=jnp.float32)
        row_dot = jnp.sum(prob_rows * d_probs, axis=-1, keepdims=True)
        d_scores = (prob_rows * (d_probs - row_dot)).astype(jnp.bfloat16)
        d_query_block = (
            jnp.einsum("hqk,khd->qhd", d_scores, key_rot, preferred_element_type=jnp.float32)
            * score_scale
        )
        key_acc = (
            key_acc
            + jnp.einsum("hqk,qhd->khd", d_scores, q_block, preferred_element_type=jnp.float32)
            * score_scale
        )
        value_acc = value_acc + jnp.einsum(
            "hqk,qhd->khd",
            prob_rows.astype(jnp.bfloat16),
            d_block,
            preferred_element_type=jnp.float32,
        )
        return ((key_acc, value_acc), d_query_block)

    zero_grads = jnp.zeros((tree_len, local_heads, HD), jnp.float32)
    (d_key_rot, d_value_acc), d_query_blocks = lax.scan(
        attend_back, (zero_grads, zero_grads), (block_starts, lse_blocks)
    )
    d_query_rot = d_query_blocks.reshape(tree_len, local_heads, HD)
    d_qpre = (
        rotate_back(d_query_rot, cosine, sine_tab)
        .reshape(tree_len, local_heads * HD)
        .astype(jnp.bfloat16)
    )
    d_kpre = (
        rotate_back(d_key_rot, cosine, sine_tab)
        .reshape(tree_len, local_heads * HD)
        .astype(jnp.bfloat16)
    )
    d_value = d_value_acc.reshape(tree_len, local_heads * HD).astype(jnp.bfloat16)
    grad_query = inner_rows(normed_all, d_qpre)
    grad_key = inner_rows(normed_all, d_kpre)
    grad_value = inner_rows(normed_all, d_value)
    d_norm_one = lax.psum_scatter(
        (
            contract_last(d_qpre, w_query)
            + contract_last(d_kpre, w_key)
            + contract_last(d_value, w_value)
        ).astype(jnp.bfloat16),
        "mp",
        scatter_dimension=0,
        tiled=True,
    ).astype(jnp.float32)
    scaled_one = gain_attn * d_norm_one
    gain_attn_part = jnp.sum(d_norm_one * inputs_f32 * inv_one, axis=0)
    input_grad = (
        d_resid
        + inv_one * scaled_one
        - inputs_f32 * inv_one**3 * jnp.mean(scaled_one * inputs_f32, axis=-1, keepdims=True)
    )
    gain_attn_grad, gain_mlp_grad = lax.psum((gain_attn_part, gain_mlp_part), ("dp", "mp"))
    grad_query, grad_key, grad_value, grad_out, grad_gate, grad_up, grad_down = lax.psum(
        (grad_query, grad_key, grad_value, grad_out, grad_gate, grad_up, grad_down), "dp"
    )
    return (
        output,
        input_grad,
        gain_attn_grad,
        grad_query,
        grad_key,
        grad_value,
        grad_out,
        gain_mlp_grad,
        grad_gate,
        grad_up,
        grad_down,
    )


def solution(mesh):
    in_specs = (
        P(("dp", "mp"), None),
        P(),
        P(None, "mp"),
        P(None, "mp"),
        P(None, "mp"),
        P("mp", None),
        P(),
        P(None, "mp"),
        P(None, "mp"),
        P("mp", None),
        P("dp", None),
        P("dp", None),
        P(("dp", "mp"), None),
    )
    out_specs = (
        P(("dp", "mp"), None),
        P(("dp", "mp"), None),
        P(),
        P(None, "mp"),
        P(None, "mp"),
        P(None, "mp"),
        P("mp", None),
        P(),
        P(None, "mp"),
        P(None, "mp"),
        P("mp", None),
    )
    return jax.shard_map(
        on_device, mesh=mesh, in_specs=in_specs, out_specs=out_specs, check_vma=False
    )
```

profile of v0, /device:TPU:0, one launch (start us, length us, event | category | flops | bytes accessed | tf_op | source)
XLA Modules:
  0.0 983.6 jit_solution(3247048086694837235)
XLA Ops:
  16.7 35.2 %all-gather.5.cloned.1.call-done = bf16[1536,768]{1,0:T(8,128)(2,1)} async-done(((bf16[768,768]{1,0:T(8,128)(2,1)}), bf16[1536,768]{1,0:T(8,128)(2,1)}) %all-gather.5.cloned.1.call-update) | async-done | bytes 2359312 | tf_op jit(solution)/shard_map/all_gather | solution.py:111
  60.2 82.5 %while.28 = (s32[]{:T(128)}, bf16[3,512,6,64]{1,3,2,0:T(8,128)(2,1)}, f32[3,6,512]{2,1,0:T(8,128)}, s32[3]{0:T(128)S(1)}, s32[1536,7]{0,1:T(8,128)}, /*index=5*/...) while((s32[]{:T(128)}, ...), condition=%wide.region_5.6_spmd.clone, body=%wide.region_2.5_spmd.clone.sunk | while | flops 1278167552 | bytes 63043776 | solution.py:135
  150.0 34.2 %reduce-scatter.5.cloned.1.call-done = bf16[768,768]{1,0:T(8,128)(2,1)} async-done(((bf16[1536,768]{1,0:T(8,128)(2,1)}), bf16[768,768]{1,0:T(8,128)(2,1)}) %reduce-scatter.5.cloned.1.call-update) | async-done | bytes 1179664 | tf_op jit(solution)/shard_map/reduce_scatter | solution.py:137
  188.6 35.6 %all-gather.7.cloned.1.call-done = bf16[1536,768]{1,0:T(8,128)(2,1)} async-done(((bf16[768,768]{1,0:T(8,128)(2,1)}), bf16[1536,768]{1,0:T(8,128)(2,1)}) %all-gather.7.cloned.1.call-update) | async-done | bytes 2359312 | tf_op jit(solution)/shard_map/all_gather | solution.py:146
  224.2 7.6 fusion.103
  236.3 25.6 %all-gather.9.cloned.1.call-done = bf16[1536,768]{1,0:T(8,128)(2,1)} async-done(((bf16[768,768]{1,0:T(8,128)(2,1)}), bf16[1536,768]{1,0:T(8,128)(2,1)}) %all-gather.9.cloned.1.call-update) | async-done | bytes 2359312 | tf_op jit(solution)/shard_map/all_gather | solution.py:158
  261.8 10.2 %multiply_convert_fusion.1 = (bf16[1536,1024]{1,0:T(8,128)(2,1)S(1)}, bf16[1536,1024]{1,0:T(8,128)(2,1)S(1)}, bf16[1536,1024]{1,0:T(8,128)(2,1)}) fusion(f32[1536,1024]{1,0:T(8,128)} %fusion.102, f32[1536,1024]{1,0:T(8,128)} %fusion.103, bf16[1536,768]{1,0:T(8,128)(2,1)} %all-gather.9.cloned.1.call-done, bf16[1024,768]{1,0:T(8,128)(2,1)S(1)} %copy-done), kind=kOutput, calls=%fused_computation.61 | convolution fusion | flops 2439512064 | bytes 25952256 | tf_op jit(solution)/shard_map/dot_general | solution.py:63
  278.8 34.8 %reduce-scatter.9.cloned.1.call-done = bf16[768,768]{1,0:T(8,128)(2,1)} async-done(((bf16[1536,768]{1,0:T(8,128)(2,1)}), bf16[768,768]{1,0:T(8,128)(2,1)}) %reduce-scatter.9.cloned.1.call-update) | async-done | bytes 1179664 | tf_op jit(solution)/shard_map/reduce_scatter | solution.py:167
  321.3 36.2 %all-gather.11.cloned.1.call-done = bf16[1536,768]{1,0:T(8,128)(2,1)} async-done(((bf16[768,768]{1,0:T(8,128)(2,1)}), bf16[1536,768]{1,0:T(8,128)(2,1)}) %all-gather.11.cloned.1.call-update) | async-done | bytes 2359312 | tf_op jit(solution)/shard_map/all_gather | solution.py:180
  361.2 243.4 %while.29 = (s32[]{:T(128)}, f32[1536,6,64]{0,2,1:T(8,128)}, f32[1536,6,64]{0,2,1:T(8,128)}, f32[3,512,6,64]{1,0,3,2:T(4,128)}, s32[3]{0:T(128)S(1)}, /*index=5*...) while((s32[]{:T(128)}, f32[1536,6,64]{0,2,1:T(8,128)}, ...), condition=%wide.region_13.14_spmd.clone, body=%wide.region_11.13_spmd.clone.sunk | while | flops 3107211776 | bytes 262388048 | solution.py:218
  382.1 7.8 fusion.210
  389.9 14.7 %multiply_reduce_fusion.3 = (f32[6,512]{1,0:T(8,128)S(1)}, f32[6,512,1536]{2,1,0:T(8,128)}) fusion(f32[6,512,1536]{2,1,0:T(8,128)} %copy-done.1, f32[6,512]{1,0:T(8,128)S(1)} %dynamic-slice_bitcast_fusion.2, pred[512,1536]{1,0:T(8,128)(4,1)S(1)} %fusion.208, bf16[1536,6,64]{0,2,1:T(8,128)(2,1)S(1)} %copy-done.8, ...), kind=kOutput, calls=%fused_computation.28.clone.1 | convolution fusion | flops 627569664 | bytes 40132612 | tf_op jit(solution)/shard_map/while/body/eval_jaxpr/qhd,khd->hqk/dot_general | solution.py:197
  404.6 13.2 %multiply_convert_fusion.6 = bf16[6,512,1536]{2,1,0:T(8,128)(2,1)S(1)} fusion(f32[6,512,1536]{2,1,0:T(8,128)} %get-tuple-element.422, f32[6,512,1536]{2,1,0:T(8,128)} %copy-done.1, f32[6,512]{1,0:T(8,128)S(1)} %get-tuple-element.423, f32[6,512]{1,0:T(8,128)S(1)} %dynamic-slice_bitcast_fusion.2, pred[512,1536]{1,0:T(8,128)(4,1)S(1)} %fusion.208), kind=kLoop, calls=%fused_computation.27.clone.1 | loop fusion | flops 28311552 | bytes 47996928 | tf_op jit(solution)/shard_map/while/body/eval_jaxpr/convert_element_type | solution.py:199
  426.0 16.1 %dynamic_update_slice.22 = f32[3,512,6,64]{1,0,3,2:T(4,128)} dynamic-update-slice(f32[3,512,6,64]{1,0,3,2:T(4,128)} %get-tuple-element.478, f32[1,512,6,64]{1,0,3,2:T(1,128)S(1)} %copy.38, s32[]{:T(128)S(6)} %copy.55, s32[]{:T(128)} %constant.41.clone.1..sunk.1, s32[]{:T(128)} %constant.41.clone.1..sunk.1, s32[]{:T(128)} %constant.41.clone.1..sunk.1) | dynamic-update-slice | bytes 1572868 | tf_op jit(solution)/shard_map/while/body/jit(dynamic_update_index_in_dim)/dynamic_update_slice | solution.py:218
  462.8 8.2 fusion.210
  471.1 14.6 %multiply_reduce_fusion.3 = (f32[6,512]{1,0:T(8,128)S(1)}, f32[6,512,1536]{2,1,0:T(8,128)}) fusion(f32[6,512,1536]{2,1,0:T(8,128)} %copy-done.1, f32[6,512]{1,0:T(8,128)S(1)} %dynamic-slice_bitcast_fusion.2, pred[512,1536]{1,0:T(8,128)(4,1)S(1)} %fusion.208, bf16[1536,6,64]{0,2,1:T(8,128)(2,1)S(1)} %copy-done.8, ...), kind=kOutput, calls=%fused_computation.28.clone.1 | convolution fusion | flops 627569664 | bytes 40132612 | tf_op jit(solution)/shard_map/while/body/eval_jaxpr/qhd,khd->hqk/dot_general | solution.py:197
  485.7 13.2 %multiply_convert_fusion.6 = bf16[6,512,1536]{2,1,0:T(8,128)(2,1)S(1)} fusion(f32[6,512,1536]{2,1,0:T(8,128)} %get-tuple-element.422, f32[6,512,1536]{2,1,0:T(8,128)} %copy-done.1, f32[6,512]{1,0:T(8,128)S(1)} %get-tuple-element.423, f32[6,512]{1,0:T(8,128)S(1)} %dynamic-slice_bitcast_fusion.2, pred[512,1536]{1,0:T(8,128)(4,1)S(1)} %fusion.208), kind=kLoop, calls=%fused_computation.27.clone.1 | loop fusion | flops 28311552 | bytes 47996928 | tf_op jit(solution)/shard_map/while/body/eval_jaxpr/convert_element_type | solution.py:199
  507.2 16.1 %dynamic_update_slice.22 = f32[3,512,6,64]{1,0,3,2:T(4,128)} dynamic-update-slice(f32[3,512,6,64]{1,0,3,2:T(4,128)} %get-tuple-element.478, f32[1,512,6,64]{1,0,3,2:T(1,128)S(1)} %copy.38, s32[]{:T(128)S(6)} %copy.55, s32[]{:T(128)} %constant.41.clone.1..sunk.1, s32[]{:T(128)} %constant.41.clone.1..sunk.1, s32[]{:T(128)} %constant.41.clone.1..sunk.1) | dynamic-update-slice | bytes 1572868 | tf_op jit(solution)/shard_map/while/body/jit(dynamic_update_index_in_dim)/dynamic_update_slice | solution.py:218
  543.9 8.2 fusion.210
  552.1 14.6 %multiply_reduce_fusion.3 = (f32[6,512]{1,0:T(8,128)S(1)}, f32[6,512,1536]{2,1,0:T(8,128)}) fusion(f32[6,512,1536]{2,1,0:T(8,128)} %copy-done.1, f32[6,512]{1,0:T(8,128)S(1)} %dynamic-slice_bitcast_fusion.2, pred[512,1536]{1,0:T(8,128)(4,1)S(1)} %fusion.208, bf16[1536,6,64]{0,2,1:T(8,128)(2,1)S(1)} %copy-done.8, ...), kind=kOutput, calls=%fused_computation.28.clone.1 | convolution fusion | flops 627569664 | bytes 40132612 | tf_op jit(solution)/shard_map/while/body/eval_jaxpr/qhd,khd->hqk/dot_general | solution.py:197
  566.7 13.2 %multiply_convert_fusion.6 = bf16[6,512,1536]{2,1,0:T(8,128)(2,1)S(1)} fusion(f32[6,512,1536]{2,1,0:T(8,128)} %get-tuple-element.422, f32[6,512,1536]{2,1,0:T(8,128)} %copy-done.1, f32[6,512]{1,0:T(8,128)S(1)} %get-tuple-element.423, f32[6,512]{1,0:T(8,128)S(1)} %dynamic-slice_bitcast_fusion.2, pred[512,1536]{1,0:T(8,128)(4,1)S(1)} %fusion.208), kind=kLoop, calls=%fused_computation.27.clone.1 | loop fusion | flops 28311552 | bytes 47996928 | tf_op jit(solution)/shard_map/while/body/eval_jaxpr/convert_element_type | solution.py:199
  588.2 16.1 %dynamic_update_slice.22 = f32[3,512,6,64]{1,0,3,2:T(4,128)} dynamic-update-slice(f32[3,512,6,64]{1,0,3,2:T(4,128)} %get-tuple-element.478, f32[1,512,6,64]{1,0,3,2:T(1,128)S(1)} %copy.38, s32[]{:T(128)S(6)} %copy.55, s32[]{:T(128)} %constant.41.clone.1..sunk.1, s32[]{:T(128)} %constant.41.clone.1..sunk.1, s32[]{:T(128)} %constant.41.clone.1..sunk.1) | dynamic-update-slice | bytes 1572868 | tf_op jit(solution)/shard_map/while/body/jit(dynamic_update_index_in_dim)/dynamic_update_slice | solution.py:218
  659.5 39.7 %all-reduce = (f32[768]{0:T(1024)}, f32[768]{0:T(1024)}) all-reduce(f32[768]{0:T(1024)S(1)} %get-tuple-element.206, f32[768]{0:T(1024)S(1)} %copy-done.47), channel_id=1, replica_groups=mesh['dp'=16,'mp'=2] {'dp','mp'}, use_global_device_ids=true, to_apply=%region_17.18 | all-reduce | flops 1536 | bytes 12288 | tf_op jit(solution)/shard_map/psum | solution.py:253
  704.3 258.5 %all-reduce.4.cloned.1.call-done = (f32[768,384]{1,0:T(8,128)}, f32[768,384]{1,0:T(8,128)}, f32[768,384]{1,0:T(8,128)}, f32[384,768]{1,0:T(8,128)}, f32[768,1024...) async-done(((f32[768,384]{1,0:T(8,128)}, f32[768,384]{1,0:T(8,128)}, f32[768,384]{1,0:T(8,128)}, f32[384,768]{1,0:T(8,128)}, f32[768,1024]{1,0:T(8,128)}, ...) | async-done | bytes 14155792 | tf_op jit(solution)/shard_map/psum | solution.py:254
  (273 shorter events, 282.2 us)
Async XLA Ops:
  7.2 254.6 %copy-start = (bf16[1024,768]{1,0:T(8,128)(2,1)S(1)}, bf16[1024,768]{1,0:T(8,128)(2,1)}, u32[]{:S(2)}) copy-start(bf16[1024,768]{1,0:T(8,128)(2,1)} %param.26) | copy-start | bytes 4718596
  7.2 44.7 %all-gather.5.cloned.1.call-start = ((), (), s32[]{:S(2)}) async-start(), calls=%async_computation.4 | async-start | bytes 3538944 | tf_op jit(solution)/shard_map/all_gather | solution.py:111
  10.2 41.6 %copy-start.30 = (bf16[768,384]{1,0:T(8,128)(2,1)S(1)}, bf16[768,384]{1,0:T(8,128)(2,1)}, u32[]{:S(2)}) copy-start(bf16[768,384]{1,0:T(8,128)(2,1)} %param.20) | copy-start | bytes 1769476
  13.0 171.2 %reduce-scatter.5.cloned.1.call-start = ((), (), s32[]{:S(2)}) async-start(), calls=%async_computation.5 | async-start | bytes 3538944 | tf_op jit(solution)/shard_map/reduce_scatter | solution.py:137
  16.7 39.3 %copy-start.19 = (f32[1536,32]{0,1:T(8,128)}, f32[1536,32]{0,1:T(8,128)S(1)}, u32[]{:S(2)}) copy-start(f32[1536,32]{0,1:T(8,128)S(1)} %get-tuple-element.280) | copy-start | bytes 589828
  16.7 39.3 %copy-start.21 = (f32[1536,32]{0,1:T(8,128)}, f32[1536,32]{0,1:T(8,128)S(1)}, u32[]{:S(2)}) copy-start(f32[1536,32]{0,1:T(8,128)S(1)} %get-tuple-element.281) | copy-start | bytes 589828
  16.7 38.1 %copy-start.28 = (bf16[768,384]{1,0:T(8,128)(2,1)S(1)}, bf16[768,384]{1,0:T(8,128)(2,1)}, u32[]{:S(2)}) copy-start(bf16[768,384]{1,0:T(8,128)(2,1)} %param.19) | copy-start | bytes 1769476
  149.3 74.9 %all-gather.7.cloned.1.call-start = ((), (), s32[]{:S(2)}) async-start(), calls=%async_computation.6 | async-start | bytes 3538944 | tf_op jit(solution)/shard_map/all_gather | solution.py:146
  150.0 167.4 %copy-start.34 = (f32[768]{0:T(1024)}, f32[768]{0:T(1024)S(1)}, u32[]{:S(2)}) copy-start(f32[768]{0:T(1024)S(1)} %convert_element_type.122) | copy-start | bytes 9220
  186.4 130.9 %copy-start.36 = (f32[768]{0:T(1024)}, f32[768]{0:T(1024)S(1)}, u32[]{:S(2)}) copy-start(f32[768]{0:T(1024)S(1)} %get-tuple-element.285) | copy-start | bytes 9220
  186.4 130.9 %copy-start.42 = (f32[768]{0:T(1024)}, f32[768]{0:T(1024)S(1)}, u32[]{:S(2)}) copy-start(f32[768]{0:T(1024)S(1)} %get-tuple-element.284) | copy-start | bytes 9220
  188.0 73.8 %all-gather.9.cloned.1.call-start = ((), (), s32[]{:S(2)}) async-start(), calls=%async_computation.8 | async-start | bytes 3538944 | tf_op jit(solution)/shard_map/all_gather | solution.py:158
  188.6 125.0 %reduce-scatter.9.cloned.1.call-start = ((), (), s32[]{:S(2)}) async-start(), calls=%async_computation.9 | async-start | bytes 3538944 | tf_op jit(solution)/shard_map/reduce_scatter | solution.py:167
  261.8 10.2 %copy-start.55 = (bf16[768,1024]{1,0:T(8,128)(2,1)S(1)}, bf16[768,1024]{1,0:T(8,128)(2,1)}, u32[]{:S(2)}) copy-start(bf16[768,1024]{1,0:T(8,128)(2,1)} %param.24) | copy-start | bytes 4718596
  278.7 78.7 %all-gather.11.cloned.1.call-start = ((), (), s32[]{:S(2)}) async-start(), calls=%async_computation.10 | async-start | bytes 3538944 | tf_op jit(solution)/shard_map/all_gather | solution.py:180
  321.2 335.9 %reduce-scatter.11.cloned.1.call-start = ((), (), s32[]{:S(2)}) async-start(), calls=%async_computation.11 | async-start | bytes 3538944 | tf_op jit(solution)/shard_map/reduce_scatter | solution.py:236
  462.8 8.3 copy-start.8
  622.2 77.0 %reduce-scatter.7.cloned.1.call-start = ((), (), s32[]{:S(2)}) async-start(), calls=%async_computation.7 | async-start | bytes 3538944 | tf_op jit(solution)/shard_map/reduce_scatter | solution.py:152
  628.2 334.6 %all-reduce.4.cloned.1.call-start = ((), (), s32[]{:S(2)}) async-start(), calls=%async_computation.12 | async-start | bytes 28311552 | tf_op jit(solution)/shard_map/psum | solution.py:254
  653.9 45.3 %copy-start.35 = (f32[768]{0:T(1024)S(1)}, f32[768]{0:T(1024)}, u32[]{:S(2)}) copy-start(f32[768]{0:T(1024)} %copy-done.34) | copy-start | bytes 9220
  653.9 45.3 %copy-start.37 = (f32[768]{0:T(1024)S(1)}, f32[768]{0:T(1024)}, u32[]{:S(2)}) copy-start(f32[768]{0:T(1024)} %copy-done.36) | copy-start | bytes 9220
  654.0 45.3 %copy-start.43 = (f32[768]{0:T(1024)S(1)}, f32[768]{0:T(1024)}, u32[]{:S(2)}) copy-start(f32[768]{0:T(1024)} %copy-done.42) | copy-start | bytes 9220
  654.0 45.3 %copy-start.45 = (f32[768]{0:T(1024)S(1)}, f32[768]{0:T(1024)}, u32[]{:S(2)}) copy-start(f32[768]{0:T(1024)} %copy-done.44) | copy-start | bytes 9220
  654.0 45.3 %copy-start.46 = (f32[768]{0:T(1024)S(1)}, f32[768]{0:T(1024)}, u32[]{:S(2)}) copy-start(f32[768]{0:T(1024)} %get-tuple-element.282) | copy-start | bytes 9220
  (57 other events, 208.0 us)
Sparse Core Ops, SparseCore 0:
  13.1 38.7 all-gather.4
  149.4 34.7 reduce-scatter.4
  188.1 36.0 all-gather.6
  225.7 36.0 all-gather.8
  278.9 34.6 reduce-scatter.8
  321.3 36.0 all-gather.10
  622.4 34.7 reduce-scatter.10
  660.0 35.1 reduce-scatter.6
  701.8 260.9 all-reduce.3
where the time goes:
time: 992 us; the launch traced here: 984 us
  waiting for transfers between devices  464 us (47%)
  matrix products  254 us (26%)
  local copies, waits for them, and re-layouts  107 us (11%)
  other arithmetic  91.1 us (9%)
  blocking collectives  39.7 us (4%)
  between operations  14.6 us (1%)
  loops' own time  13.3 us (1%)
    psum x1, waiting for transfers between devices, on_device(): lax.psum((grad_query, grad_key, grad_value, grad_out, grad_gate, grad_up,...  258 us
    dynamic_update_slice x6, local copies, waits for them, and re-layouts, on_device(): lax.scan(attend_back, (zero_grads, zero_grads), (block_starts, lse_blocks))  50.6 us
    dot_general x3, matrix products, attend_back(): jnp.einsum('qhd,khd->hqk', d_block, values, preferred_element_type=jnp.fl...  43.8 us
    psum x1, blocking collectives, on_device(): lax.psum((gain_attn_part, gain_mlp_part), ('dp', 'mp'))  39.7 us
    convert_element_type x3, other arithmetic, attend_back(): d_scores = (prob_rows * (d_probs - row_dot)).astype(jnp.bfloat16)  39.7 us
    dot_general x6, matrix products, block_mask(): jnp.dot(vis_block, onehot.T) > 0  38.2 us
    all_gather x1, waiting for transfers between devices, on_device(): lax.all_gather(d_resid.astype(jnp.bfloat16), 'mp', axis=0, tiled=True)  36.2 us
    all_gather x1, waiting for transfers between devices, on_device(): normed_two_all = lax.all_gather(normed_two, 'mp', axis=0, tiled=True)  35.6 us
  transfers between devices with their start and end apart: 9, of which 8 were waited for; matrix products, arithmetic and copies ran while one was open for 6% of the time, Pallas kernels for 0%

commit v1 on v0

v1 whole, which is shorter than its diff:
```python
import functools
import math

import jax
import jax.numpy as jnp
from jax import lax
from jax.experimental import pallas as pl
from jax.experimental.pallas import tpu as pltpu
from jax.sharding import Mesh
from jax.sharding import PartitionSpec as P

BF = jnp.bfloat16
F32 = jnp.float32
HD=64; EPS=1e-5; BIG=-1e30
C_Q = (HD**-0.5)*math.log2(math.e)
LN2 = math.log(2.0)
NT=(((1,),(1,)),((),())); NN=(((1,),(0,)),((),())); TN=(((0,),(0,)),((),()))
def dot(a,b,dims=NN): return lax.dot_general(a,b,dims,preferred_element_type=F32)
def lanes(shape): return lax.broadcasted_iota(jnp.int32, shape, 1)

def split3(x):
    hi=x.astype(BF).astype(F32); r=x-hi; mid=r.astype(BF).astype(F32); lo=r-mid
    return hi,mid,lo

def tables(starts, parents, row0, rows, nseg, tree_len):
    sh=(rows,128)
    t = row0 + lax.broadcasted_iota(jnp.int32, sh, 0)
    st=[starts[0,s] for s in range(nseg)]+[tree_len]
    par=[parents[0,s] for s in range(nseg)]
    ln=[st[s+1]-st[s] for s in range(nseg)]
    def pick(vals, idx):
        r = vals[0]
        for s in range(1,nseg): r = jnp.where(idx==s, vals[s], r)
        return r
    D=[]
    gps=[]
    for s in range(nseg):
        p=par[s]; gp=pick(par,p); gps.append(gp)
        off=jnp.where(p!=s, pick(ln,p), 0)+jnp.where((gp!=s)&(gp!=p), pick(ln,gp), 0)
        D.append(off-st[s])
    seg=jnp.zeros(sh,jnp.int32); pos=t+D[0]
    for s in range(1,nseg):
        ge=t>=st[s]
        seg=seg+ge.astype(jnp.int32)
        pos=pos+jnp.where(ge, D[s]-D[s-1], 0)
    f=lanes(sh)-64
    parl=jnp.zeros((1,128),jnp.int32)-1; gpl=parl
    fl=lanes((1,128))-64
    for s in range(nseg):
        parl=jnp.where(fl==s, par[s], parl); gpl=jnp.where(fl==s, gps[s], gpl)
    vis=(f==seg)|(parl==seg)|(gpl==seg)|(f<0)|(f>=nseg)
    qf=jnp.where(f==seg,1.0,0.0)
    kf=jnp.where(vis,0.0,BIG)
    kf=jnp.where((f>=8)&(f<11),1.0,kf)
    return pos.astype(F32), qf, kf

def rot_tables(posf):
    l=lax.broadcasted_iota(jnp.int32,(1,128),1)
    fr=jnp.exp((l%32).astype(F32)*(-2.0*math.log(10000.0)/HD))
    ang=posf*fr
    sg=jnp.where((l%64)<32,-1.0,1.0)
    return jnp.cos(ang), jnp.sin(ang)*sg

def swap32(x):
    l=lanes(x.shape)
    return jnp.where((l&32)==0, pltpu.roll(x,96,1), pltpu.roll(x,32,1))

def fwd_kernel(nseg, starts, parents, x_ref, gain, wq, wk, wv, normed, heads, qe, ke, ve, cos_o, sin_o):
    T=x_ref.shape[0]; R=256; nh=wq.shape[1]//HD
    def proj(c,_):
        r0=pl.multiple_of(c*R,R); rows=pl.ds(r0,R)
        x=x_ref[rows,:].astype(F32)
        r1=lax.rsqrt(jnp.mean(x*x,axis=1,keepdims=True)+EPS)
        n=(x*r1*gain[...].astype(F32)).astype(BF)
        normed[rows,:]=n
        posf,qf,kf=tables(starts,parents,r0,R,nseg,T)
        co,si=rot_tables(posf)
        cos_o[rows,:]=co; sin_o[rows,:]=si
        l=lanes((R,128)); low=l<64
        vone=jnp.where((l>=64)&(l<67),1.0,0.0)
        for p in range(nh//2):
            cs=slice(128*p,128*p+128)
            q=dot(n,wq[:,cs]); k=dot(n,wk[:,cs]); v=dot(n,wv[:,cs])
            q=(q*co+swap32(q)*si)*C_Q; k=k*co+swap32(k)*si
            for hh in range(2):
                if hh: q=pltpu.roll(q,64,1); k=pltpu.roll(k,64,1); v=pltpu.roll(v,64,1)
                qe[2*p+hh,rows,:]=jnp.where(low,q,qf).astype(BF)
                ke[2*p+hh,rows,:]=jnp.where(low,k,kf).astype(BF)
                ve[2*p+hh,rows,:]=jnp.where(low,v,vone).astype(BF)
        return 0
    lax.fori_loop(0,T//R,proj,0)
    B=256
    causal=lax.broadcasted_iota(jnp.int32,(B,B),1)<=lax.broadcasted_iota(jnp.int32,(B,B),0)
    l=lanes((B,128))
    def attend(p,_):
        for i in range(T//B):
            n=(i+1)*B; rows=slice(i*B,(i+1)*B)
            outs=[]
            for hh in range(2):
                h=2*p+hh
                q=qe[h,rows,:]
                s=dot(q,ke[h,0:n,:],NT)
                sd=jnp.where(causal,s[:,n-B:],BIG)
                s=sd if i==0 else jnp.concatenate([s[:,:n-B],sd],axis=1)
                m=jnp.max(s,axis=1,keepdims=True)
                pr=jnp.exp2(s-m).astype(BF)
                o=dot(pr,ve[h,0:n,:])
                den=o[:,64:65]
                o=o*(1.0/den)
                lse=m+jnp.log2(den)
                a,b,c=split3(-lse)
                qq=jnp.where(l==72,a,jnp.where(l==73,b,jnp.where(l==74,c,q.astype(F32))))
                qe[h,rows,:]=qq.astype(BF)
                outs.append(o)
            heads_p=jnp.where(l<64,outs[0],pltpu.roll(outs[1],64,1)).astype(BF)
            heads[rows,pl.ds(pl.multiple_of(p*128,128),128)]=heads_p
        return 0
    lax.fori_loop(0,nh//2,attend,0)

def attn_fwd(x_all, gain, wq, wk, wv, starts, parents):
    T,Dm=x_all.shape; H=wq.shape[1]; nh=H//HD; nseg=starts.shape[1]
    V=pl.BlockSpec(memory_space=pltpu.VMEM); S=pl.BlockSpec(memory_space=pltpu.SMEM)
    sd=jax.ShapeDtypeStruct
    return pl.pallas_call(functools.partial(fwd_kernel,nseg),
        out_shape=(sd((T,Dm),BF), sd((T,H),BF), sd((nh,T,128),BF), sd((nh,T,128),BF), sd((nh,T,128),BF), sd((T,128),F32), sd((T,128),F32)),
        in_specs=[S,S,V,V,V,V,V], out_specs=(V,)*7,
        compiler_params=pltpu.CompilerParams(vmem_limit_bytes=60*2**20), name="attn_fwd",
        )(starts, parents, x_all, gain.reshape(1,-1), wq, wk, wv)

def bwd_kernel(heads, dh_ref, qe, ke, ve, cos_o, sin_o, dq_ref, dk_ref, dv_ref, doe, kt, dqt):
    T=qe.shape[1]; nh=qe.shape[0]; B=256; nb=T//B
    l=lanes((B,128)); low=l<64
    causal=lax.broadcasted_iota(jnp.int32,(B,B),0)<=lax.broadcasted_iota(jnp.int32,(B,B),1)
    def pair(p,_):
        cols=pl.ds(pl.multiple_of(p*128,128),128)
        for i in range(nb):
            rows=slice(i*B,(i+1)*B)
            d=dh_ref[rows,cols].astype(F32); o=heads[rows,cols].astype(F32)
            t=d*o
            for hh in range(2):
                if hh: t=pltpu.roll(t,64,1); d=pltpu.roll(d,64,1)
                delta=jnp.sum(jnp.where(low,t,0.0),axis=1,keepdims=True)
                a,b,c=split3(-delta)
                doe[hh,rows,:]=jnp.where(low,d,jnp.where(l==64,a,jnp.where(l==65,b,jnp.where(l==66,c,0.0)))).astype(BF)
                kt[hh,:,rows]=ke[2*p+hh,rows,:].T[0:64]
        dqt[...]=jnp.zeros_like(dqt)
        for j in range(nb):
            ks=slice(j*B,(j+1)*B); n0=j*B
            res=[]
            for hh in range(2):
                h=2*p+hh
                s=dot(ke[h,ks,:],qe[h,n0:,:],NT)
                dp=dot(ve[h,ks,:],doe[hh,n0:,:],NT)
                sd=jnp.where(causal,s[:,:B],BIG)
                s=sd if j==nb-1 else jnp.concatenate([sd,s[:,B:]],axis=1)
                pt=jnp.exp2(s)
                ds=(pt*dp).astype(BF)
                pt=pt.astype(BF)
                dv=dot(pt,doe[hh,n0:,:])
                dk=dot(ds,qe[h,n0:,:])*LN2
                dqt[64*hh:64*hh+64,n0:]+=dot(kt[hh,:,ks],ds)
                res.append((dk,dv))
            dk=jnp.where(low,res[0][0],pltpu.roll(res[1][0],64,1))
            dv=jnp.where(low,res[0][1],pltpu.roll(res[1][1],64,1))
            co=cos_o[ks,:]; si=sin_o[ks,:]
            dk_ref[ks,cols]=(dk*co-swap32(dk)*si).astype(BF)
            dv_ref[ks,cols]=dv.astype(BF)
        for i in range(nb):
            rows=slice(i*B,(i+1)*B)
            dq=dqt[:,rows].T*(HD**-0.5)
            co=cos_o[rows,:]; si=sin_o[rows,:]
            dq_ref[rows,cols]=(dq*co-swap32(dq)*si).astype(BF)
        return 0
    lax.fori_loop(0,nh//2,pair,0)

def attn_bwd(heads, dh, qe, ke, ve, co, si):
    nh,T,_=qe.shape
    V=pl.BlockSpec(memory_space=pltpu.VMEM); sd=jax.ShapeDtypeStruct
    return pl.pallas_call(bwd_kernel,
        out_shape=(sd(heads.shape,BF),)*3,
        in_specs=[V]*7, out_specs=(V,)*3,
        scratch_shapes=[pltpu.VMEM((2,T,128),BF),pltpu.VMEM((2,64,T),BF),pltpu.VMEM((128,T),F32)],
        compiler_params=pltpu.CompilerParams(vmem_limit_bytes=60*2**20), name="attn_bwd",
        )(heads, dh, qe, ke, ve, co, si)

MESH=pl.DeviceIdType.MESH
RING=8
def ring_chip(r):
    half=RING//2
    return jnp.where(r<half, 2*r, 2*(RING-1-r)+1)
def chip_ring(n):
    return jnp.where(n%2==0, n//2, RING-1-n//2)

class Reducer:
    def __init__(self, own, peer, r1o, r1p, asend, r2, bs, slots, fin, outs, sems, segs):
        self.__dict__.update(locals())
        self.core=lax.axis_index("core"); self.mp=lax.axis_index("mp"); self.chip=lax.axis_index("chip")
        self.pos=chip_ring(self.chip)
        self.nxt=[ring_chip(lax.rem(self.pos+1,RING)), ring_chip(lax.rem(self.pos+RING-1,RING))]
        self.na=len(own)
    def barrier(self):
        b=pltpu.get_barrier_semaphore()
        for d in self.peers(): pl.semaphore_signal(b, inc=1, device_id=d, device_id_type=MESH)
        pl.semaphore_wait(b, len(self.peers()))
    def peers(self):
        p=[{"core":1-self.core},{"chip":self.nxt[0]},{"chip":self.nxt[1]}]
        if self.peer: p.append({"mp":1-self.mp})
        return p
    def cp(self, src, dst, k, dev):
        s=self.sems
        return pltpu.make_async_remote_copy(src,dst,s.at[0,k],s.at[1,k],device_id=dev,device_id_type=MESH)
    def c_core(self,a,which):
        o=1-self.core
        src=(self.own if which==0 else self.peer)[a].at[o]; dst=(self.r1o if which==0 else self.r1p)[a]
        return self.cp(src,dst,which*self.na+a,{"core":o})
    def c_x(self,a): return self.cp(self.asend[a],self.r2[a],2*self.na+a,{"mp":1-self.mp})
    def chunk(self,d,t):
        return lax.rem(self.pos-t+2*RING,RING) if d==0 else lax.rem(self.pos+t,RING)
    def c_rs(self,i,t):
        a,r0,nr,d=self.segs[i]
        ch=self.chunk(d,t+1)
        src=self.bs[a].at[ch,pl.ds(r0,nr)] if t==0 else self.slots[i].at[t-1]
        return self.cp(src,self.slots[i].at[t],3*self.na+i*14+t,{"chip":self.nxt[d]})
    def c_ag(self,i,t):
        a,r0,nr,d=self.segs[i]
        ch=self.chunk(d,t)
        ref=self.fin[a].at[self.core,ch,pl.ds(r0,nr)]
        return self.cp(ref,ref,3*self.na+i*14+7+t,{"chip":self.nxt[d]})
    def c_fin(self,a):
        ref=self.fin[a].at[self.core]
        return self.cp(ref,ref,3*self.na+len(self.segs)*14+a,{"core":1-self.core})
    @staticmethod
    def nsem(na,nseg): return 3*na+nseg*14+na
    def ticks(self):
        na=self.na; R=range(na); I=range(len(self.segs)); out=[]
        def start():
            for a in R:
                if self.peer: self.c_core(a,1).start()
            for a in R: self.c_core(a,0).start()
        out.append(start)
        if self.peer:
            def x(a):
                def f():
                    self.c_core(a,1).wait()
                    self.asend[a][...]=(self.peer[a][self.core].astype(F32)+self.r1p[a][...].astype(F32)).astype(BF)
                    self.c_x(a).start()
                return f
            out+= [x(a) for a in R]
        def b(a):
            def f():
                self.c_core(a,0).wait()
                v=self.own[a][self.core].astype(F32)+self.r1o[a][...].astype(F32)
                if self.peer:
                    self.c_x(a).wait()
                    v=v+self.r2[a][...].astype(F32)
                self.bs[a][...]=v.astype(BF)
            return f
        def first():
            for a in R: b(a)()
            for i in I: self.c_rs(i,0).start()
        out.append(first)
        def rs(t):
            def f():
                for i in I:
                    a,r0,nr,d=self.segs[i]
                    self.c_rs(i,t).wait()
                    ch=self.chunk(d,t+2)
                    v=(self.slots[i][t].astype(F32)+self.bs[a][ch,pl.ds(r0,nr)].astype(F32)).astype(BF)
                    if t<RING-2:
                        self.slots[i][t]=v
                        self.c_rs(i,t+1).start()
                    else:
                        self.fin[a][self.core,self.pos,pl.ds(r0,nr)]=v
                        self.c_ag(i,0).start()
            return f
        out+=[rs(t) for t in range(RING-1)]
        def ag(t):
            def f():
                for i in I:
                    self.c_ag(i,t).wait()
                    if t<RING-2: self.c_ag(i,t+1).start()
            return f
        out+=[ag(t) for t in range(RING-1)]
        def fin():
            for a in R: self.c_fin(a).start()
            def put(a,c):
                self.outs[a][c]=self.fin[a][c].astype(F32)
            for a in R: put(a,self.core)
            for a in R:
                self.c_fin(a).wait(); put(a,1-self.core)
        out.append(fin)
        return out

def scratch(shapes, segs, peer):
    V=lambda s,d=BF: pltpu.VMEM(s,d)
    n=len(shapes); sc=[]
    sc+=[V((RING,r,c)) for r,c in shapes]
    if peer:
        sc+=[V((RING,r,c)) for r,c in shapes]*3
    sc+=[V((RING,r,c)) for r,c in shapes]
    sc+=[V((RING-1,nr,shapes[a][1])) for a,_,nr,_ in segs]
    sc+=[V((2,RING,r,c)) for r,c in shapes]
    sc+=[pltpu.SemaphoreType.DMA((2,Reducer.nsem(n,len(segs))))]
    return sc
def unpack(own,peer,outs,sc,segs):
    n=len(own); sc=list(sc)
    def take(k):
        r=sc[:k]; del sc[:k]; return r
    r1o=take(n)
    r1p=asend=r2=None
    if peer: r1p=take(n); asend=take(n); r2=take(n)
    bs=take(n); slots=take(len(segs)); fin=take(n); sems=sc[0]
    return Reducer(own,peer,r1o,r1p,asend,r2,bs,slots,fin,outs,sems,segs)

def ar_kernel(n,has_peer,segs,*refs):
    own=refs[:n]; k=n
    peer=refs[n:2*n] if has_peer else None
    if has_peer: k=2*n
    outs=refs[k:k+n]; sc=refs[k+n:]
    rd=unpack(own,peer,outs,sc,segs)
    rd.barrier()
    for t in rd.ticks(): t()

def all_reduce(own, peer, segs, cid):
    n=len(own); shapes=[a.shape[2:] for a in own]
    V=pl.BlockSpec(memory_space=pltpu.VMEM)
    args=list(own)+(list(peer) if peer else [])
    return pl.pallas_call(functools.partial(ar_kernel,n,bool(peer),segs),
        out_shape=tuple(jax.ShapeDtypeStruct(a.shape,F32) for a in own),
        in_specs=[V]*len(args), out_specs=(V,)*n,
        scratch_shapes=scratch(shapes,segs,bool(peer)),
        compiler_params=pltpu.CompilerParams(collective_id=cid,has_side_effects=True,vmem_limit_bytes=63*2**20),
        name="grad_reduce")(*args)
SEG1=[(0,0,48,0),(1,0,48,1),(2,0,32,0),(2,32,32,1),(3,0,48,0)]
SEG2=[(0,0,48,0),(1,0,48,1),(2,0,16,0),(2,16,32,1),(3,0,16,0)]

PAIR = [(0, 1), (1, 0)]


def swap(v, axis):
    return lax.ppermute(v, axis, PAIR)


def rms_scale(vectors):
    return lax.rsqrt(jnp.mean(vectors * vectors, axis=-1, keepdims=True) + EPS)


def on_device(layer_input, gain_attn, w_query, w_key, w_value, w_out, gain_mlp, w_gate, w_up, w_down,
              segment_start, segment_parent, out_grad):
    rows, width = layer_input.shape
    core, mp = lax.axis_index("core"), lax.axis_index("mp")
    x_peer = swap(layer_input, "mp")
    first = mp == 0
    x_all = jnp.where(first, jnp.concatenate([layer_input, x_peer]), jnp.concatenate([x_peer, layer_input]))

    def other_half(w):
        half = w.shape[0] // 2
        mine = lax.dynamic_slice_in_dim(w, core * half, half, 0)
        mine, _ = lax.optimization_barrier((mine, x_peer))
        got = swap(mine, "mp")
        rest = swap(got, "core")
        return jnp.where(core == 0, jnp.concatenate([got, rest]), jnp.concatenate([rest, got]))

    peer_out, peer_gate, peer_up, peer_down = (other_half(w) for w in (w_out, w_gate, w_up, w_down))

    normed, heads, qe, ke, ve, cosine, sine = attn_fwd(
        x_all, gain_attn, w_query, w_key, w_value, segment_start, segment_parent
    )
    mine_at, peer_at = mp * rows, (1 - mp) * rows
    heads_own = lax.dynamic_slice_in_dim(heads, mine_at, rows, 0)
    heads_peer = swap(lax.dynamic_slice_in_dim(heads, peer_at, rows, 0), "mp")
    inputs = layer_input.astype(F32)
    residual = inputs + dot(heads_own, w_out) + dot(heads_peer, peer_out)
    inv_two = rms_scale(residual)
    normed_two = (residual * inv_two * gain_mlp).astype(BF)
    output = residual
    d_norm_two = 0.0
    grads = []
    for gate_w, up_w, down_w in ((w_gate, w_up, w_down), (peer_gate, peer_up, peer_down)):
        gate, up = dot(normed_two, gate_w), dot(normed_two, up_w)
        sig = jax.nn.sigmoid(gate)
        silu = gate * sig
        hidden = (silu * up).astype(BF)
        output = output + dot(hidden, down_w)
        d_hidden = dot(out_grad, down_w, NT)
        d_gate = (d_hidden * up * sig * (1.0 + gate * (1.0 - sig))).astype(BF)
        d_up = (d_hidden * silu).astype(BF)
        d_norm_two = d_norm_two + dot(d_gate, gate_w, NT) + dot(d_up, up_w, NT)
        grads.append([dot(normed_two, d_gate, TN), dot(normed_two, d_up, TN), dot(hidden, out_grad, TN)])
    scaled_two = gain_mlp * d_norm_two
    gain_mlp_part = jnp.sum(d_norm_two * residual * inv_two, axis=0)
    d_resid = (
        out_grad.astype(F32)
        + inv_two * scaled_two
        - residual * inv_two**3 * jnp.mean(scaled_two * residual, axis=-1, keepdims=True)
    )
    d_attn = d_resid.astype(BF)
    dh_peer = swap(dot(d_attn, peer_out, NT).astype(BF), "mp")
    dh_own = dot(d_attn, w_out, NT).astype(BF)
    grads[0].append(dot(d_attn, heads_own, TN))
    grads[1].append(dot(d_attn, heads_peer, TN))
    d_heads = jnp.where(first, jnp.concatenate([dh_own, dh_peer]), jnp.concatenate([dh_peer, dh_own]))
    d_qpre, d_kpre, d_value = attn_bwd(heads, d_heads, qe, ke, ve, cosine, sine)
    partial = dot(d_qpre, w_query, NT) + dot(d_kpre, w_key, NT) + dot(d_value, w_value, NT)
    theirs = lax.dynamic_slice_in_dim(partial, peer_at, rows, 0).astype(BF)
    d_norm_one = lax.dynamic_slice_in_dim(partial, mine_at, rows, 0) + swap(theirs, "mp").astype(F32)
    inv_one = rms_scale(inputs)
    scaled_one = gain_attn * d_norm_one
    gain_attn_part = jnp.sum(d_norm_one * inputs * inv_one, axis=0)
    input_grad = (
        d_resid
        + inv_one * scaled_one
        - inputs * inv_one**3 * jnp.mean(scaled_one * inputs, axis=-1, keepdims=True)
    )

    def blocks(g):
        if lax.axis_size("grp") > 1:
            g = lax.psum(g, "grp")
        return g.astype(BF).reshape(2, RING, -1, g.shape[-1])

    def whole(g):
        return g.reshape(-1, g.shape[-1])

    mlp = all_reduce([blocks(g) for g in grads[0]], [blocks(g) for g in grads[1]], SEG1, 1)
    gains = jnp.concatenate([gain_attn_part, gain_mlp_part])
    gains = gains + swap(gains, "mp")
    if lax.axis_size("grp") > 1:
        gains = lax.psum(gains, "grp")
    gains = jnp.pad(gains.reshape(2, RING, 1, -1), ((0, 0), (0, 0), (0, 15), (0, 0)))
    gains = jnp.pad(gains, ((0, 0), (0, 0), (0, 0), (0, 128 - gains.shape[-1]))).astype(BF)
    qkv = [dot(normed, d, TN) for d in (d_qpre, d_kpre, d_value)]
    qkv = all_reduce([blocks(g) for g in qkv] + [gains], None, SEG2, 2)
    gains = qkv[3][:, :, 0, : 2 * width // (2 * RING)].reshape(2, width)
    return (
        output, input_grad, gains[0], whole(qkv[0]), whole(qkv[1]), whole(qkv[2]), whole(mlp[3]).T,
        gains[1], whole(mlp[0]), whole(mlp[1]), whole(mlp[2]),
    )


def solution(mesh):
    fine = Mesh(mesh.devices.reshape(-1, RING, 2, mesh.shape["mp"]), ("grp", "chip", "core", "mp"))
    dp = ("grp", "chip", "core")
    tok, col, row, tree = P(dp + ("mp",), None), P(None, "mp"), P("mp", None), P(dp, None)
    in_specs = (tok, P(), col, col, col, row, P(), col, col, row, tree, tree, tok)
    out_specs = (tok, tok, P(), col, col, col, row, P(), col, col, row)
    return jax.shard_map(on_device, mesh=fine, in_specs=in_specs, out_specs=out_specs, check_vma=False)
```

time: 992 us -> 471 us (0.47)
  waiting for transfers between devices: 464 us -> 63.7 us
  Pallas kernels: 0 us -> 269 us
  matrix products: 254 us -> 64.6 us
  other arithmetic: 91.1 us -> 10.9 us
  local copies, waits for them, and re-layouts: 107 us -> 40.7 us
  blocking collectives: 39.7 us -> 0 us
  loops' own time: 13.3 us -> 0 us
  starting transfers between devices: 0.54 us -> 13.8 us
  between operations: 14.6 us -> 1.66 us
    pallas_call x0 -> x4, Pallas kernels: none -> 269 us  [the longest x2 205 us: all_reduce(): pl.pallas_call(functools.partial(ar_kernel, n, bool(peer), segs), out_sha...]
    psum x1 -> x0, waiting for transfers between devices: 258 us -> none  [on_device(): lax.psum((grad_query, grad_key, grad_value, grad_out, grad_gate, grad_up,...]
    dot_general x52 -> x30, matrix products: 254 us -> 64.6 us  [dot(): return lax.dot_general(a, b, dims, preferred_element_type=F32)]
    all_gather x4 -> x0, waiting for transfers between devices: 132 us -> none  [the longest x1 36.2 us: on_device(): lax.all_gather(d_resid.astype(jnp.bfloat16), 'mp', axis=0, tiled=True)]
    reduce_scatter x4 -> x0, waiting for transfers between devices: 72.1 us -> none  [the longest x1 34.8 us: on_device(): lax.psum_scatter((contract_last(d_gate, w_gate) + contract_last(d_up, w_u...]
    ppermute x0 -> x13, waiting for transfers between devices: none -> 63.7 us  [swap(): return lax.ppermute(v, axis, PAIR)]
    dynamic_update_slice x6 -> x0, local copies, waits for them, and re-layouts: 50.6 us -> none  [on_device(): lax.scan(attend_back, (zero_grads, zero_grads), (block_starts, lse_blocks))]
    convert_element_type x10 -> x4, other arithmetic: 49.8 us -> 1.49 us  [the longest x1 0.65 us: on_device(): d_attn = d_resid.astype(BF)]
  transfers between devices with their start and end apart: 9 -> 13, of which waited for: 8 -> 5; matrix products, arithmetic and copies ran while one was open for 6% -> 14% of each run, Pallas kernels for 0% -> 33%
where the time goes in v1:
time: 471 us; the launch traced here: 464 us
  Pallas kernels  269 us (57%)
  matrix products  64.6 us (14%)
  waiting for transfers between devices  63.7 us (14%)
  local copies, waits for them, and re-layouts  40.7 us (9%)
  starting transfers between devices  13.8 us (3%)
  other arithmetic  10.9 us (2%)
    pallas_call x2, Pallas kernels, all_reduce(): pl.pallas_call(functools.partial(ar_kernel, n, bool(peer), segs), out_sha...  205 us
    dot_general x30, matrix products, dot(): return lax.dot_general(a, b, dims, preferred_element_type=F32)  64.6 us
    ppermute x13, waiting for transfers between devices, swap(): return lax.ppermute(v, axis, PAIR)  63.7 us
    pallas_call x1, Pallas kernels, attn_fwd(): pl.pallas_call(functools.partial(fwd_kernel, nseg), out_shape=(sd((T, Dm)...  33.8 us
    pallas_call x1, Pallas kernels, attn_bwd(): pl.pallas_call(bwd_kernel, out_shape=(sd(heads.shape, BF),) * 3, in_specs...  30.5 us
    unnamed x92, local copies, waits for them, and re-layouts  25.7 us
    ppermute x13, starting transfers between devices, swap(): return lax.ppermute(v, axis, PAIR)  13.8 us
  transfers between devices with their start and end apart: 13, of which 5 were waited for; matrix products, arithmetic and copies ran while one was open for 14% of the time, Pallas kernels for 33%

profile of v1, /device:TPU:0, one launch (start us, length us, event | category | flops | bytes accessed | tf_op | source)
XLA Modules:
  0.0 464.1 jit_solution(8123611865299865207)
XLA Ops:
  0.7 3.0 collective-permute-start
  6.7 2.7 constant_dynamic-slice_fusion.1
  9.7 20.1 %collective-permute-done = bf16[768,768]{1,0:T(8,128)(2,1)S(1)} collective-permute-done((bf16[768,768]{1,0:T(8,128)(2,1)}, bf16[768,768]{1,0:T(8,128)(2,1)S(1)}, u32[]{:S(2)}, u32[]{:S(2)}) %collective-permute-start) | collective-permute-done | bytes 1179680 | tf_op jit(solution)/shard_map/ppermute | solution.py:341
  31.6 33.8 %attn_fwd.1 = (bf16[1536,768]{1,0:T(8,128)(2,1)}, bf16[1536,384]{1,0:T(8,128)(2,1)}, bf16[6,1536,128]{2,1,0:T(8,128)(2,1)}, bf16[6,1536,128]{2,1,0:T(8,128)(2,1)...) custom-call(s32[1,7]{1,0:T(1,128)} %starts.1, s32[1,7]{1,0:T(1,128)} %parents.1, ...), custom_call_target="tpu_custom_call" | custom-call | tf_op jit(solution)/shard_map/attn_fwd/pallas_call | solution.py:124
  78.2 12.0 %collective-permute-done.2 = bf16[192,768]{1,0:T(8,128)(2,1)} collective-permute-done((bf16[192,768]{1,0:T(8,128)(2,1)}, bf16[192,768]{1,0:T(8,128)(2,1)}, u32[]{:S(2)}, u32[]{:S(2)}) %collective-permute-start.2) | collective-permute-done | bytes 294944 | tf_op jit(solution)/shard_map/ppermute | solution.py:341
  99.7 3.3 multiply_convert_fusion
  105.8 2.6 convolution_convert_fusion.5
  113.0 10.8 %collective-permute-done.6 = bf16[384,1024]{1,0:T(8,128)(2,1)S(1)} collective-permute-done((bf16[384,1024]{1,0:T(8,128)(2,1)}, bf16[384,1024]{1,0:T(8,128)(2,1)S(1)}, u32[]{:S(2)}, u32[]{:S(2)}) %collective-permute-start.6) | collective-permute-done | bytes 786464 | tf_op jit(solution)/shard_map/ppermute | solution.py:341
  123.8 2.6 convolution_convert_fusion.3
  126.4 12.5 %collective-permute-done.8 = bf16[512,768]{1,0:T(8,128)(2,1)S(1)} collective-permute-done((bf16[512,768]{1,0:T(8,128)(2,1)}, bf16[512,768]{1,0:T(8,128)(2,1)S(1)}, u32[]{:S(2)}, u32[]{:S(2)}) %collective-permute-start.8) | collective-permute-done | bytes 786464 | tf_op jit(solution)/shard_map/ppermute | solution.py:341
  141.9 4.1 fusion.3
  145.9 2.6 convolution_convert_fusion.2
  148.6 2.6 convolution_convert_fusion.1
  152.6 2.6 multiply_reduce_fusion
  160.7 2.7 convolution_convert_fusion
  166.7 8.3 %collective-permute-done.10 = bf16[768,384]{1,0:T(8,128)(2,1)S(1)} collective-permute-done((bf16[768,384]{1,0:T(8,128)(2,1)S(1)}, bf16[768,384]{1,0:T(8,128)(2,1)S(1)}, u32[]{:S(2)}, u32[]{:S(2)}) %collective-permute-start.10) | collective-permute-done | bytes 589856 | tf_op jit(solution)/shard_map/ppermute | solution.py:341
  176.5 30.5 %attn_bwd.1 = (bf16[1536,384]{1,0:T(8,128)(2,1)}, bf16[1536,384]{1,0:T(8,128)(2,1)}, bf16[1536,384]{1,0:T(8,128)(2,1)}) custom-call(bf16[1536,384]{1,0:T(8,128)(2,1)} %get-tuple-element.33.heads, bf16[1536,384]{1,0:T(8,128)(2,1)} %maximum_select_fusion.4.dh_ref, bf16[6,1536,128]{2,1,0:T(8,128)(2,1)} %get-tuple-element.38.qe, ...), custom_call_target="tpu_custom_call" | custom-call | tf_op jit(solution)/shard_map/attn_bwd/pallas_call | solution.py:179
  207.0 2.8 fusion.37
  221.2 151.4 %grad_reduce.3 = (f32[2,8,48,1024]{3,2,1,0:T(8,128)}, f32[2,8,48,1024]{3,2,1,0:T(8,128)}, f32[2,8,64,768]{3,2,1,0:T(8,128)}, f32[2,8,48,384]{3,2,1,0:T(8,128)}) custom-call(bf16[2,8,48,1024]{3,2,1,0:T(8,128)(2,1)} %bitcast.85, bf16[2,8,48,1024]{3,2,1,0:T(8,128)(2,1)} %bitcast.86, bf16[2,8,64,768]{3,2,1,0:T(8,128)(2,1)} %bitcast.87, ...), custom_call_target="tpu_custom_call" | custom-call | tf_op jit(solution)/shard_map/grad_reduce/pallas_call | solution.py:328
  372.7 2.7 copy.52
  375.5 4.0 convolution_convert_fusion.8
  379.5 4.0 convolution_convert_fusion.7
  390.0 2.7 fusion.9
  395.4 53.1 %grad_reduce.2 = (f32[2,8,48,384]{3,2,1,0:T(8,128)}, f32[2,8,48,384]{3,2,1,0:T(8,128)}, f32[2,8,48,384]{3,2,1,0:T(8,128)}, f32[2,8,16,128]{3,2,1,0:T(8,128)}) custom-call(bf16[2,8,48,384]{3,2,1,0:T(8,128)(2,1)} %bitcast.96, bf16[2,8,48,384]{3,2,1,0:T(8,128)(2,1)} %bitcast.97, bf16[2,8,48,384]{3,2,1,0:T(8,128)(2,1)} %bitcast.98, ...), custom_call_target="tpu_custom_call" | custom-call | tf_op jit(solution)/shard_map/grad_reduce/pallas_call | solution.py:328
  (156 shorter events, 84.9 us)
Async XLA Ops:
  0.6 5.3 %copy-start = (bf16[384,768]{1,0:T(8,128)(2,1)S(1)}, bf16[384,768]{1,0:T(8,128)(2,1)}, u32[]{:S(2)}) copy-start(bf16[384,768]{1,0:T(8,128)(2,1)} %param.18) | copy-start | bytes 1769476
  0.7 29.2 %collective-permute-start = (bf16[768,768]{1,0:T(8,128)(2,1)}, bf16[768,768]{1,0:T(8,128)(2,1)S(1)}, u32[]{:S(2)}, u32[]{:S(2)}) collective-permute-start(bf16[768,768]{1,0:T(8,128)(2,1)} %param.13), channel_id=1, source_target_pairs={{0,1},{1,0},{2,3},{3,2},{4,5},{5,4},{6,7},{7,6},{8,9},{9,8},{10,11... | collective-permute-start | bytes 3538952 | tf_op jit(solution)/shard_map/ppermute | solution.py:341
  5.3 86.8 %copy-start.4 = (bf16[768,768]{0,1:T(8,128)(2,1)}, bf16[768,768]{0,1:T(8,128)(2,1)S(1)}, u32[]{:S(2)}) copy-start(bf16[768,768]{0,1:T(8,128)(2,1)S(1)} %copy.39) | copy-start | bytes 3538948
  6.7 23.2 %copy-start.11 = (bf16[768,768]{1,0:T(8,128)(2,1)S(1)}, bf16[768,768]{1,0:T(8,128)(2,1)}, u32[]{:S(2)}) copy-start(bf16[768,768]{1,0:T(8,128)(2,1)} %param.13) | copy-start | bytes 3538948
  65.3 6.7 %copy-start.37 = (bf16[768]{0:T(1024)(128)(2,1)S(1)}, bf16[768]{0:T(1024)(128)(2,1)}, u32[]{:S(2)}) copy-start(bf16[768]{0:T(1024)(128)(2,1)} %param.19) | copy-start | bytes 4612
  67.3 24.8 %collective-permute-start.1 = (bf16[768,384]{1,0:T(8,128)(2,1)}, bf16[768,384]{1,0:T(8,128)(2,1)S(1)}, u32[]{:S(2)}, u32[]{:S(2)}) collective-permute-start(bf16[768,384]{1,0:T(8,128)(2,1)} %constant_dynamic-slice_fusion.4), channel_id=1, source_target_pairs={{0,1},{1,0},{2,3},{3,2},{4,5},{5,4},{6,7},{7,6},{8,9},{9,8},{10,11... | collective-permute-start | bytes 1769480 | tf_op jit(solution)/shard_map/ppermute | solution.py:341
  69.0 21.2 %collective-permute-start.2 = (bf16[192,768]{1,0:T(8,128)(2,1)}, bf16[192,768]{1,0:T(8,128)(2,1)}, u32[]{:S(2)}, u32[]{:S(2)}) collective-permute-start(bf16[192,768]{1,0:T(8,128)(2,1)} %constant_dynamic-slice_fusion.3), channel_id=1, source_target_pairs={{0,1},{1,0},{2,3},{3,2},{4,5},{5,4},{6,7},{7,6},{8,9},{9,8},{10,11... | collective-permute-start | bytes 884744 | tf_op jit(solution)/shard_map/ppermute | solution.py:341
  73.8 81.4 %copy-start.7 = (bf16[768,768]{0,1:T(8,128)(2,1)}, bf16[768,768]{0,1:T(8,128)(2,1)S(1)}, u32[]{:S(2)}) copy-start(bf16[768,768]{0,1:T(8,128)(2,1)S(1)} %copy.42) | copy-start | bytes 3538948
  74.5 33.9 %collective-permute-start.4 = (bf16[384,1024]{1,0:T(8,128)(2,1)}, bf16[384,1024]{1,0:T(8,128)(2,1)S(1)}, u32[]{:S(2)}, u32[]{:S(2)}) collective-permute-start(bf16[384,1024]{1,0:T(8,128)(2,1)} %get-tuple-element.35), channel_id=1, source_target_pairs={{0,1},{1,0},{2,3},{3,2},{4,5},{5,4},{6,7},{7,6},{8,9},{9,8},{10,11... | collective-permute-start | bytes 2359304 | tf_op jit(solution)/shard_map/ppermute | solution.py:341
  76.2 47.6 %collective-permute-start.6 = (bf16[384,1024]{1,0:T(8,128)(2,1)}, bf16[384,1024]{1,0:T(8,128)(2,1)S(1)}, u32[]{:S(2)}, u32[]{:S(2)}) collective-permute-start(bf16[384,1024]{1,0:T(8,128)(2,1)} %get-tuple-element.36), channel_id=1, source_target_pairs={{0,1},{1,0},{2,3},{3,2},{4,5},{5,4},{6,7},{7,6},{8,9},{9,8},{10,11... | collective-permute-start | bytes 2359304 | tf_op jit(solution)/shard_map/ppermute | solution.py:341
  76.5 62.4 %collective-permute-start.8 = (bf16[512,768]{1,0:T(8,128)(2,1)}, bf16[512,768]{1,0:T(8,128)(2,1)S(1)}, u32[]{:S(2)}, u32[]{:S(2)}) collective-permute-start(bf16[512,768]{1,0:T(8,128)(2,1)} %constant_dynamic-slice_fusion), channel_id=1, source_target_pairs={{0,1},{1,0},{2,3},{3,2},{4,5},{5,4},{6,7},{7,6},{8,9},{9,8},{10,11... | collective-permute-start | bytes 2359304 | tf_op jit(solution)/shard_map/ppermute | solution.py:341
  90.2 1.9 collective-permute-start.3
  94.2 70.9 %copy-start.2 = (f32[768,768]{0,1:T(8,128)}, f32[768,768]{0,1:T(8,128)S(1)}, u32[]{:S(2)}) copy-start(f32[768,768]{0,1:T(8,128)S(1)} %get-tuple-element.94) | copy-start | bytes 7077892
  108.4 30.5 %collective-permute-start.5 = (bf16[384,1024]{1,0:T(8,128)(2,1)S(1)}, bf16[384,1024]{1,0:T(8,128)(2,1)S(1)}, u32[]{:S(2)}, u32[]{:S(2)}) collective-permute-start(bf16[384,1024]{1,0:T(8,128)(2,1)S(1)} %collective-permute-done.4), channel_id=1, source_target_pairs={{0,2},{2,0},{1,3},{3,1},{4,6},{6,4},{5,7},{7,5},{8,10},{10,8},{9,1... | collective-permute-start | bytes 2359304 | tf_op jit(solution)/shard_map/ppermute | solution.py:341
  123.8 16.6 %collective-permute-start.7 = (bf16[384,1024]{1,0:T(8,128)(2,1)S(1)}, bf16[384,1024]{1,0:T(8,128)(2,1)S(1)}, u32[]{:S(2)}, u32[]{:S(2)}) collective-permute-start(bf16[384,1024]{1,0:T(8,128)(2,1)S(1)} %collective-permute-done.6), channel_id=1, source_target_pairs={{0,2},{2,0},{1,3},{3,1},{4,6},{6,4},{5,7},{7,5},{8,10},{10,8},{9,1... | collective-permute-start | bytes 2359304 | tf_op jit(solution)/shard_map/ppermute | solution.py:341
  138.9 3.0 collective-permute-start.9
  156.5 6.9 %copy-start.22 = (bf16[768,768]{0,1:T(8,128)(2,1)}, bf16[768,768]{0,1:T(8,128)(2,1)S(1)}, u32[]{:S(2)}) copy-start(bf16[768,768]{0,1:T(8,128)(2,1)S(1)} %fusion.31) | copy-start | bytes 3538948
  159.3 15.8 %collective-permute-start.10 = (bf16[768,384]{1,0:T(8,128)(2,1)S(1)}, bf16[768,384]{1,0:T(8,128)(2,1)S(1)}, u32[]{:S(2)}, u32[]{:S(2)}) collective-permute-start(bf16[768,384]{1,0:T(8,128)(2,1)S(1)} %convolution_convert_fusion.11), channel_id=1, source_target_pairs={{0,1},{1,0},{2,3},{3,2},{4,5},{5,4},{6,7},{7,6},{8,9},{9,8},{10,11... | collective-permute-start | bytes 1769480 | tf_op jit(solution)/shard_map/ppermute | solution.py:341
  176.5 30.5 %copy-start.16 = (bf16[768,384]{1,0:T(8,128)(2,1)S(1)}, bf16[768,384]{1,0:T(8,128)(2,1)}, u32[]{:S(2)}) copy-start(bf16[768,384]{1,0:T(8,128)(2,1)} %wq.1) | copy-start | bytes 1769476
  216.1 169.8 %collective-permute-start.11 = (bf16[768,768]{0,1:T(8,128)(2,1)}, bf16[768,768]{0,1:T(8,128)(2,1)}, u32[]{:S(2)}, u32[]{:S(2)}) collective-permute-start(bf16[768,768]{0,1:T(8,128)(2,1)} %dynamic-slice_convert_fusion), channel_id=1, source_target_pairs={{0,1},{1,0},{2,3},{3,2},{4,5},{5,4},{6,7},{7,6},{8,9},{9,8},{10,11... | collective-permute-start | bytes 3538952 | tf_op jit(solution)/shard_map/ppermute | solution.py:341
  375.5 10.4 %slice-start = ((s8[4718592]{0:T(1024)(128)(4,1)}), s8[4194304]{0:T(1024)(128)(4,1)S(1)}, s32[]{:S(2)}) async-start(s8[4718592]{0:T(1024)(128)(4,1)} %bitcast.80), calls=%async_computation | async-start | bytes 8388608
  379.5 6.3 %slice-start.1 = ((s8[4718592]{0:T(1024)(128)(4,1)}), s8[524288]{0:T(1024)(128)(4,1)S(1)}, s32[]{:S(2)}) async-start(s8[4718592]{0:T(1024)(128)(4,1)} %bitcast.80), calls=%async_computation.1 | async-start | bytes 1048576
  383.6 6.4 %copy-start.10 = (f32[768,768]{0,1:T(8,128)S(1)}, f32[768,768]{0,1:T(8,128)}, u32[]{:S(2)}) copy-start(f32[768,768]{0,1:T(8,128)} %copy-done.9) | copy-start | bytes 7077892
  388.5 6.2 %collective-permute-start.12 = (f32[1536]{0:T(1024)S(1)}, f32[1536]{0:T(1024)S(1)}, u32[]{:S(2)}, u32[]{:S(2)}) collective-permute-start(f32[1536]{0:T(1024)S(1)} %pad_maximum_fusion), channel_id=1, source_target_pairs={{0,1},{1,0},{2,3},{3,2},{4,5},{5,4},{6,7},{7,6},{8,9},{9,8},{10,11... | collective-permute-start | bytes 18440 | tf_op jit(solution)/shard_map/ppermute | solution.py:341
  (30 other events, 84.2 us)
